TPU v7x, 128 devices: a whole 4x4x4 slice. The times are simulated.
128 devices in a mesh: grp: 16 (over y, x), lag: 8 (over z, core).
Axes of the slice: x: 4, y: 4, z: 4, core: 2. Of those that a mesh axis runs over, the one named last changes fastest.
Arguments:
- weights: bfloat16 [3, 16384, 256], P(None, 'lag'), may hold values from -0.125 to 0.125
- history: bfloat16 [512, 2048, 256], P(('grp', 'lag')), may hold values from -6 to 6
- send_patch: int32 [2048, 2], P(('grp', 'lag')), may hold values from 0 to 3
- send_lag: int32 [2048, 2], P(('grp', 'lag')), may hold values from 0 to 56
- send_class: int32 [2048, 2], P(('grp', 'lag')), may hold values from 0 to 2
- recv_target: int32 [2048, 2], P(('grp', 'lag')), may hold values from 0 to 3
- local_src: int32 [6144], P(('grp', 'lag')), may hold values from 0 to 3
- local_lag: int32 [6144], P(('grp', 'lag')), may hold values from 0 to 56
- local_class: int32 [6144], P(('grp', 'lag')), may hold values from 0 to 2
- local_target: int32 [6144], P(('grp', 'lag')), may hold values from 0 to 3
- inverse_blocks: bfloat16 [512, 256, 256], P(('grp', 'lag')), may hold values from -0.375 to 0.375
- incident: bfloat16 [512, 256, 256], P(('grp', 'lag')), may hold values from -6 to 6
Outputs:
- density: bfloat16 [512, 256, 256], P(('grp', 'lag'))
All inputs are finite; a program needn't handle non-finite values.
Results may differ from a plain program's by a relative error of at most 0.0049.
Values may be sent and summed in bfloat16 or wider, within the bound.
A program may use at most 256 MiB of HBM per device.

v0:
```python
import jax
import jax.numpy as jnp
from jax import lax
from jax.sharding import PartitionSpec as P


def pair_product(gathered, source, key, klass, offset):
    panel_count = gathered.shape[2]
    height = source.shape[1]
    window = lax.dynamic_slice(
        gathered, (klass, offset * panel_count, jnp.int32(0)), (1, height, panel_count)
    )[0]
    rows = lax.dynamic_index_in_dim(source, key, 0, keepdims=False)
    return lax.dot_general(
        window, rows, (((0,), (0,)), ((), ())), preferred_element_type=jnp.float32
    )


def block_width():
    return 8


def block_products(gathered, source, block_keys, block_classes, block_offsets):
    outputs = [
        pair_product(gathered, source, block_keys[i], block_classes[i], block_offsets[i])
        for i in range(block_keys.shape[0])
    ]
    return jnp.stack(outputs, 0)


def compute_pairs(gathered, source, keys, classes, offsets):
    total = keys.shape[0]
    width = block_width()

    def compute_step(carry, inputs):
        block_keys, block_classes, block_offsets = inputs
        return (carry, block_products(gathered, source, block_keys, block_classes, block_offsets))

    _, result = lax.scan(
        compute_step,
        jnp.int32(0),
        (keys.reshape(-1, width), classes.reshape(-1, width), offsets.reshape(-1, width)),
    )
    return result.reshape(total, result.shape[2], result.shape[3])


def collect(owned, targets, contrib):
    select = (jnp.arange(owned, dtype=jnp.int32)[:, None] == targets[None, :]).astype(jnp.float32)
    return jnp.einsum("ts,spc->tpc", select, contrib, precision=lax.Precision.HIGHEST)


def accumulate_pairs(gathered, source, keys, classes, offsets, targets, initial):
    width = block_width()
    owned = initial.shape[0]

    def accumulate_step(carry, inputs):
        block_keys, block_classes, block_offsets, block_targets = inputs
        contrib = block_products(gathered, source, block_keys, block_classes, block_offsets)
        return (carry + collect(owned, block_targets, contrib), None)

    result, _ = lax.scan(
        accumulate_step,
        initial,
        (
            keys.reshape(-1, width),
            classes.reshape(-1, width),
            offsets.reshape(-1, width),
            targets.reshape(-1, width),
        ),
    )
    return result


def per_device(
    weights,
    history,
    send_patch,
    send_lag,
    send_class,
    recv_target,
    local_src,
    local_lag,
    local_class,
    local_target,
    inverse_blocks,
    incident,
):
    owned = history.shape[0]
    panel_count = weights.shape[2]
    excite = history.shape[2]
    peers = send_patch.shape[0]
    slots = send_patch.shape[1]
    gathered = lax.all_gather(weights, "lag", axis=1, tiled=True)
    computed = compute_pairs(
        gathered,
        history,
        send_patch.reshape(peers * slots),
        send_class.reshape(peers * slots),
        send_lag.reshape(peers * slots),
    )
    remote = lax.all_to_all(
        computed.reshape(peers, slots, panel_count, excite),
        "grp",
        split_axis=0,
        concat_axis=0,
        tiled=True,
    )
    near_start = jnp.zeros((owned, panel_count, excite), jnp.float32)
    near_sum = accumulate_pairs(
        gathered, history, local_src, local_class, local_lag, local_target, near_start
    )
    near_sum = near_sum + collect(
        owned,
        recv_target.reshape(peers * slots),
        remote.reshape(peers * slots, panel_count, excite),
    )
    residual = (incident.astype(jnp.float32) - near_sum).astype(jnp.bfloat16)
    density = jnp.einsum(
        "tpq,tqc->tpc", inverse_blocks, residual, preferred_element_type=jnp.float32
    )
    return density.astype(jnp.bfloat16)


def solution(mesh):
    return jax.shard_map(
        per_device,
        mesh=mesh,
        in_specs=(
            P(None, "lag", None),
            P(("grp", "lag"), None, None),
            P(("grp", "lag"), None),
            P(("grp", "lag"), None),
            P(("grp", "lag"), None),
            P(("grp", "lag"), None),
            P(("grp", "lag")),
            P(("grp", "lag")),
            P(("grp", "lag")),
            P(("grp", "lag")),
            P(("grp", "lag"), None, None),
            P(("grp", "lag"), None, None),
        ),
        out_specs=P(("grp", "lag"), None, None),
        check_vma=False,
    )
```

profile of v0, /device:TPU:1, one launch (start us, length us, event | category | flops | bytes accessed | tf_op | source)
XLA Modules:
  0.0 721.8 jit_solution(8559357001827942845)
XLA Ops:
  13.6 119.5 %all-gather.2.cloned.1.call-done = bf16[3,16384,256]{2,1,0:T(8,128)(2,1)} async-done(((bf16[3,2048,256]{2,1,0:T(8,128)(2,1)}), bf16[3,16384,256]{2,1,0:T(8,128)(2,1)}) %all-gather.2.cloned.1.call-update) | async-done | bytes 25165840 | tf_op jit(solution)/shard_map/all_gather | solution.py:93
  133.1 216.0 %while.21 = (s32[]{:T(128)}, f32[4,8,256,256]{3,2,1,0:T(8,128)}, s32[4,8]{1,0:T(4,128)S(1)}, s32[4,8]{1,0:T(4,128)S(1)}, bf16[3,16384,256]{2,1,0:T(8,128)(2,1)},...) while((s32[]{:T(128)}, f32[4,8,256,256]{3,2,1,0:T(8,128)}, ...), condition=%wide.region_3.4_spmd, body=%wide.region_2.3_spmd.sunk | while | flops 2147483648 | bytes 23070708 | solution.py:39
  145.8 2.0 fusion.206
  152.0 2.0 fusion.207
  158.1 2.0 fusion.208
  164.6 2.0 fusion.209
  171.0 2.0 fusion.210
  177.2 2.0 fusion.211
  183.6 2.0 fusion.212
  199.7 2.0 fusion.206
  206.0 2.0 fusion.207
  212.1 2.0 fusion.208
  218.6 2.0 fusion.209
  225.0 2.0 fusion.210
  231.2 2.0 fusion.211
  237.6 2.0 fusion.212
  260.0 2.0 fusion.207
  272.6 2.0 fusion.209
  279.0 2.0 fusion.210
  291.6 2.0 fusion.212
  307.8 2.0 fusion.206
  320.1 2.0 fusion.208
  326.6 2.0 fusion.209
  333.0 2.0 fusion.210
  345.6 2.0 fusion.212
  349.1 6.6 all-to-all-start
  355.7 346.6 %while.22 = (s32[]{:T(128)}, f32[4,256,256]{2,0,1:T(4,128)}, s32[6,8]{1,0:T(8,128)S(1)}, s32[6,8]{1,0:T(8,128)S(1)}, s32[6,8]{1,0:T(8,128)S(1)}, /*index=5*/bf16...) while((s32[]{:T(128)}, f32[4,256,256]{2,0,1:T(4,128)}, ...), condition=%wide.region_1.2_spmd.clone, body=%wide.region_0.1_spmd.clone.sunk | while | flops 2173173760 | bytes 23070312 | solution.py:61
  375.3 2.0 fusion.236
  381.8 2.0 fusion.237
  388.1 2.0 fusion.238
  400.6 2.0 fusion.240
  407.1 2.0 fusion.241
  409.1 3.4 fusion.243
  432.0 2.0 fusion.236
  438.6 2.0 fusion.237
  444.9 2.0 fusion.238
  457.3 2.0 fusion.240
  463.8 2.0 fusion.241
  465.9 4.6 fusion.243
  490.0 2.0 fusion.236
  496.6 2.0 fusion.237
  502.8 2.0 fusion.238
  515.3 2.0 fusion.240
  521.8 2.0 fusion.241
  523.9 4.6 fusion.243
  547.9 2.0 fusion.236
  554.5 2.0 fusion.237
  560.8 2.0 fusion.238
  573.2 2.0 fusion.240
  579.8 2.0 fusion.241
  581.8 4.6 fusion.243
  605.9 2.0 fusion.236
  612.5 2.0 fusion.237
  618.8 2.0 fusion.238
  631.2 2.0 fusion.240
  637.7 2.0 fusion.241
  639.8 4.6 fusion.243
  663.9 2.0 fusion.236
  670.4 2.0 fusion.237
  676.7 2.0 fusion.238
  689.1 2.0 fusion.240
  695.7 2.0 fusion.241
  697.7 4.6 fusion.243
  702.3 11.2 %fusion.113 = bf16[4,256,256]{2,0,1:T(4,128)(2,1)S(1)} fusion(f32[4,256,256]{2,0,1:T(4,128)} %get-tuple-element.84, f32[32,256,256]{2,1,0:T(8,128)} %bitcast.51, bf16[4,256,256]{2,1,0:T(8,128)(2,1)S(1)} %copy-done.1, s32[32]{0:T(128)S(1)} %eq.31), kind=kOutput, calls=%fused_computation.131 | convolution fusion | flops 101712000 | bytes 10485888 | tf_op jit(solution)/shard_map/ts,spc->tpc/dot_general | solution.py:49
  (110 shorter events, 89.4 us)
Async XLA Ops:
  6.5 707.0 %copy-start = (bf16[4,256,256]{2,1,0:T(8,128)(2,1)S(1)}, bf16[4,256,256]{2,1,0:T(8,128)(2,1)}, u32[]{:S(2)}) copy-start(bf16[4,256,256]{2,1,0:T(8,128)(2,1)} %param.26) | copy-start | bytes 1572868
  6.5 126.6 %all-gather.2.cloned.1.call-start = ((), (), s32[]{:S(2)}) async-start(), calls=%async_computation.1 | async-start | bytes 28311552 | tf_op jit(solution)/shard_map/all_gather | solution.py:93
  349.1 353.2 %all-to-all-start = ((f32[16,2,256,256]{3,2,1,0:T(8,128)}), f32[16,2,256,256]{3,2,1,0:T(8,128)}, u32[]{:S(2)}, u32[]{:S(2)}) async-start(f32[16,2,256,256]{3,2,1,0:T(8,128)} %bitcast.421), calls=%async_computation | async-start | bytes 16777216 | tf_op jit(solution)/shard_map/all_to_all | solution.py:101
  355.7 346.6 %copy-start.1 = (bf16[4,256,256]{2,1,0:T(8,128)(2,1)S(1)}, bf16[4,256,256]{2,1,0:T(8,128)(2,1)}, u32[]{:S(2)}) copy-start(bf16[4,256,256]{2,1,0:T(8,128)(2,1)} %param.27) | copy-start | bytes 1572868
Sparse Core Ops, SparseCore 0:
  9.1 124.0 all-gather.1
where the time goes:
time: 730 us; the launch traced here: 722 us
  loops' own time  348 us (48%)
  matrix products  200 us (27%)
  waiting for transfers between devices  120 us (16%)
  local copies, waits for them, and re-layouts  33.7 us (5%)
  between operations  13.4 us (2%)
    another operation x1, loops' own time, accumulate_pairs(): lax.scan(accumulate_step, initial, (keys.reshape(-1, width), classes.resh...  211 us
    dot_general x80, matrix products, pair_product(): lax.dot_general(window, rows, (((0,), (0,)), ((), ())), preferred_element...  162 us
    another operation x1, loops' own time, compute_pairs(): lax.scan(compute_step, jnp.int32(0), (keys.reshape(-1, width), classes.re...  137 us
    all_gather x1, waiting for transfers between devices, per_device(): gathered = lax.all_gather(weights, 'lag', axis=1, tiled=True)  120 us
    dot_general x7, matrix products, collect(): jnp.einsum('ts,spc->tpc', select, contrib, precision=lax.Precision.HIGHEST)  37.5 us
  transfers between devices with their start and end apart: 2, of which 1 were waited for; matrix products, arithmetic and copies ran while one was open for 20% of the time, Pallas kernels for 0%

commit v1 on v0

--- a/solution.py
+++ b/solution.py
@@ -90,7 +90,9 @@
     excite = history.shape[2]
     peers = send_patch.shape[0]
     slots = send_patch.shape[1]
-    gathered = lax.all_gather(weights, "lag", axis=1, tiled=True)
+    gathered = jnp.concatenate(
+        lax.all_to_all(jnp.stack([weights] * lax.axis_size("lag")), "lag", 0, 0), axis=1
+    )
     computed = compute_pairs(
         gathered,
         history,

time: 730 us -> 936 us (1.28)
  waiting for transfers between devices: 120 us -> 272 us
  local copies, waits for them, and re-layouts: 33.7 us -> 94.1 us
  between operations: 13.4 us -> 0.09 us
    all_to_all x0 -> x1, waiting for transfers between devices: none -> 272 us  [per_device(): lax.all_to_all(jnp.stack([weights] * lax.axis_size('lag')), 'lag', 0, 0)]
    all_gather x1 -> x0, waiting for transfers between devices: 120 us -> none  [per_device(): gathered = lax.all_gather(weights, 'lag', axis=1, tiled=True)]
    all_to_all x0 -> x2, local copies, waits for them, and re-layouts: none -> 29.1 us  [the longest x1 20.5 us: per_device(): lax.all_to_all(jnp.stack([weights] * lax.axis_size('lag')), 'lag', 0, 0)]
    another operation x0 -> x2, local copies, waits for them, and re-layouts: none -> 25.1 us  [the longest x1 15.4 us: per_device(): computed.reshape(peers, slots, panel_count, excite)]
    reshape x0 -> x1, local copies, waits for them, and re-layouts: none -> 11 us  [per_device(): remote.reshape(peers * slots, panel_count, excite)]
  transfers between devices with their start and end apart: 2 -> 2, of which waited for: 1 -> 1; matrix products, arithmetic and copies ran while one was open for 20% -> 15% of each run, Pallas kernels for 0% -> 0%
where the time goes in v1:
time: 936 us; the launch traced here: 928 us
  loops' own time  351 us (38%)
  waiting for transfers between devices  272 us (29%)
  matrix products  195 us (21%)
  local copies, waits for them, and re-layouts  94.1 us (10%)
  starting transfers between devices  14.7 us (2%)
    all_to_all x1, waiting for transfers between devices, per_device(): lax.all_to_all(jnp.stack([weights] * lax.axis_size('lag')), 'lag', 0, 0)  272 us
    another operation x1, loops' own time, accumulate_pairs(): lax.scan(accumulate_step, initial, (keys.reshape(-1, width), classes.resh...  212 us
    dot_general x80, matrix products, pair_product(): lax.dot_general(window, rows, (((0,), (0,)), ((), ())), preferred_element...  162 us
    another operation x1, loops' own time, compute_pairs(): lax.scan(compute_step, jnp.int32(0), (keys.reshape(-1, width), classes.re...  139 us
    dot_general x7, matrix products, collect(): jnp.einsum('ts,spc->tpc', select, contrib, precision=lax.Precision.HIGHEST)  32.7 us
    all_to_all x1, local copies, waits for them, and re-layouts, per_device(): lax.all_to_all(jnp.stack([weights] * lax.axis_size('lag')), 'lag', 0, 0)  20.5 us
  transfers between devices with their start and end apart: 2, of which 1 were waited for; matrix products, arithmetic and copies ran while one was open for 15% of the time, Pallas kernels for 0%

profile of v1, /device:TPU:1, one launch (start us, length us, event | category | flops | bytes accessed | tf_op | source)
XLA Modules:
  0.0 927.6 jit_solution(14118013440880205926)
XLA Ops:
  0.0 9.7 %stack.65 = bf16[8,3,2048,256]{3,2,1,0:T(8,128)(2,1)} broadcast(bf16[3,2048,256]{2,1,0:T(8,128)(2,1)} %param.16), dimensions={1,2,3} | broadcast | bytes 28311552 | tf_op jit(solution)/shard_map/stack | solution.py:94
  9.8 7.9 all-to-all-start
  18.7 272.4 %all-to-all-done = bf16[8,3,2048,256]{3,2,1,0:T(8,128)(2,1)} async-done(((bf16[8,3,2048,256]{3,2,1,0:T(8,128)(2,1)}), bf16[8,3,2048,256]{3,2,1,0:T(8,128)(2,1)}, u32[]{:S(2)}, u32[]{:S(2)}) %all-to-all-start) | async-done | bytes 25165856 | tf_op jit(solution)/shard_map/all_to_all | solution.py:94
  291.2 20.5 %copy.60 = bf16[8,3,2048,256]{3,2,0,1:T(8,128)(2,1)} copy(bf16[8,3,2048,256]{3,2,1,0:T(8,128)(2,1)} %all-to-all-done) | data formatting | bytes 50331648 | tf_op jit(solution)/shard_map/all_to_all | solution.py:94
  311.7 218.6 %while.21 = (s32[]{:T(128)}, f32[4,8,256,256]{3,2,1,0:T(8,128)}, s32[4,8]{1,0:T(4,128)S(1)}, s32[4,8]{1,0:T(4,128)S(1)}, bf16[3,16384,256]{2,1,0:T(8,128)(2,1)},...) while((s32[]{:T(128)}, f32[4,8,256,256]{3,2,1,0:T(8,128)}, ...), condition=%wide.region_3.4_spmd, body=%wide.region_2.3_spmd.sunk | while | flops 2147483648 | bytes 23070708 | solution.py:39
  324.8 2.0 fusion.198
  330.9 2.0 fusion.199
  337.6 2.0 fusion.200
  350.2 2.0 fusion.202
  362.7 2.0 fusion.204
  385.5 2.0 fusion.199
  392.2 2.0 fusion.200
  404.9 2.0 fusion.202
  417.3 2.0 fusion.204
  434.1 2.0 fusion.198
  440.2 2.0 fusion.199
  446.9 2.0 fusion.200
  459.6 2.0 fusion.202
  472.0 2.0 fusion.204
  488.8 2.0 fusion.198
  494.8 2.0 fusion.199
  514.2 2.0 fusion.202
  526.7 2.0 fusion.204
  530.3 15.4 %copy.65 = f32[16,2,256,256]{3,1,2,0:T(2,128)} copy(f32[16,2,256,256]{3,2,1,0:T(8,128)} %bitcast.427) | data formatting | bytes 16777216 | tf_op jit(solution)/shard_map/reshape;reshape | solution.py:104
  545.7 6.8 all-to-all-start.1
  552.5 347.6 %while.22 = (s32[]{:T(128)}, f32[4,256,256]{2,0,1:T(4,128)}, s32[6,8]{1,0:T(8,128)S(1)}, s32[6,8]{1,0:T(8,128)S(1)}, s32[6,8]{1,0:T(8,128)S(1)}, /*index=5*/bf16...) while((s32[]{:T(128)}, f32[4,256,256]{2,0,1:T(4,128)}, ...), condition=%wide.region_1.2_spmd.clone, body=%wide.region_0.1_spmd.clone.sunk | while | flops 2173173760 | bytes 23070312 | solution.py:61
  565.3 2.0 fusion.227
  578.1 2.0 fusion.229
  584.3 2.0 fusion.230
  597.7 2.0 fusion.232
  604.0 2.0 fusion.233
  606.1 3.3 fusion.235
  622.2 2.0 fusion.227
  628.6 2.0 fusion.228
  641.2 2.0 fusion.230
  654.6 2.0 fusion.232
  660.9 2.0 fusion.233
  663.0 4.6 fusion.235
  680.3 2.0 fusion.227
  686.7 2.0 fusion.228
  693.1 2.0 fusion.229
  699.3 2.0 fusion.230
  712.7 2.0 fusion.232
  719.1 2.0 fusion.233
  721.1 4.6 fusion.235
  738.4 2.0 fusion.227
  757.4 2.0 fusion.230
  770.8 2.0 fusion.232
  777.2 2.0 fusion.233
  779.3 4.6 fusion.235
  796.5 2.0 fusion.227
  803.0 2.0 fusion.228
  809.4 2.0 fusion.229
  815.6 2.0 fusion.230
  835.3 2.0 fusion.233
  837.4 4.6 fusion.235
  854.7 2.0 fusion.227
  873.7 2.0 fusion.230
  887.1 2.0 fusion.232
  893.4 2.0 fusion.233
  895.5 4.6 fusion.235
  900.1 8.6 copy.66
  908.7 11.0 %reshape.158 = f32[32,256,256]{2,0,1:T(8,128)} reshape(f32[16,2,256,256]{3,1,0,2:T(2,128)} %copy.66) | data formatting | bytes 16777216 | tf_op jit(solution)/shard_map/reshape | solution.py:117
  919.7 6.5 fusion.106
  (132 shorter events, 96.1 us)
Async XLA Ops:
  0.0 926.2 %copy-start = (bf16[4,256,256]{2,1,0:T(8,128)(2,1)S(1)}, bf16[4,256,256]{2,1,0:T(8,128)(2,1)}, u32[]{:S(2)}) copy-start(bf16[4,256,256]{2,1,0:T(8,128)(2,1)} %param.26) | copy-start | bytes 1572868
  9.7 8.0 copy-start.3
  9.8 8.1 copy-start.4
  9.8 8.3 copy-start.5
  9.8 8.5 copy-start.7
  9.8 8.5 copy-start.8
  9.8 8.6 copy-start.9
  9.8 8.7 copy-start.10
  9.8 8.7 copy-start.6
  9.8 281.4 %all-to-all-start = ((bf16[8,3,2048,256]{3,2,1,0:T(8,128)(2,1)}), bf16[8,3,2048,256]{3,2,1,0:T(8,128)(2,1)}, u32[]{:S(2)}, u32[]{:S(2)}) async-start(bf16[8,3,2048,256]{3,2,1,0:T(8,128)(2,1)} %stack.65), calls=%async_computation | async-start | bytes 50331648 | tf_op jit(solution)/shard_map/all_to_all | solution.py:94
  545.7 354.4 %all-to-all-start.1 = ((f32[16,2,256,256]{3,1,2,0:T(2,128)}), f32[16,2,256,256]{3,1,2,0:T(2,128)}, u32[]{:S(2)}, u32[]{:S(2)}) async-start(f32[16,2,256,256]{3,1,2,0:T(2,128)} %copy.65), calls=%async_computation.1 | async-start | bytes 16777216 | tf_op jit(solution)/shard_map/all_to_all | solution.py:103
  908.7 11.0 %copy-start.1 = (f32[4,256,256]{2,0,1:T(4,128)S(1)}, f32[4,256,256]{2,0,1:T(4,128)}, u32[]{:S(2)}) copy-start(f32[4,256,256]{2,0,1:T(4,128)} %get-tuple-element.84) | copy-start | bytes 3145732
  908.7 11.0 %copy-start.2 = (bf16[4,256,256]{2,1,0:T(8,128)(2,1)S(1)}, bf16[4,256,256]{2,1,0:T(8,128)(2,1)}, u32[]{:S(2)}) copy-start(bf16[4,256,256]{2,1,0:T(8,128)(2,1)} %param.27) | copy-start | bytes 1572868
